TPU v7x, 32 devices: a whole 2x2x4 slice. The times are simulated.
32 devices in a mesh: row: 4 (over z), col: 8 (over y, x, core).
Axes of the slice: x: 2, y: 2, z: 4, core: 2. Of those that a mesh axis runs over, the one named last changes fastest.
Arguments:
- x_blocks: bfloat16 [1024, 1024, 128], P('row', 'col'), may hold values from -0.0625 to 0.0625
- block_ids: int32 [1024, 8], P('row', 'col'), may hold values from 0 to 511, as said below
- margins: float32 [16384], P('row'), may hold values from -6 to 6
- deleted: int32 [2048], P('row'), may hold values from 0 to 16383, as said below
- grads: float32 [16384, 128], P('col'), may hold values from -6 to 6
Outputs:
- solution: float32 [16384, 128], P('col')
- residual: float32 [16384, 128], P('col')
Inputs may be any that keep to these rules, and one draw needn't show every extreme that they name: `block_ids`: each device's 256 entries are distinct and rise; each device lists the first and the last block of its grid. `deleted`: the 512 entries of row shard r are distinct rows of that shard, r * 4096 and up; each shard deletes its first and its last row.
All inputs are finite; a program needn't handle non-finite values.
Results may differ from a plain program's by a relative error of at most 0.015.
Values may be sent and summed in bfloat16 or wider, within the bound.
No kernel may reach another device: no remote copies, remote signals or barrier semaphores. Data moves between devices by JAX's collectives and lax.ppermute only.
A program may use at most 128 MiB of HBM per device.

v0:
```python
import jax
import jax.numpy as jnp
from jax import lax
from jax.sharding import PartitionSpec as P

ITERS = 3
highest = lax.Precision.HIGHEST
ridge_weight = 0.2


def on_device(x_blocks, block_ids, margins, deleted, grads):
    block_width = x_blocks.shape[1]
    feature_rows = grads.shape[0]
    directions = grads.shape[1]
    row_count = margins.shape[0]
    row_blocks = row_count // block_width
    feature_blocks = feature_rows // block_width
    pattern = block_ids[:, 0]
    block_row = pattern // feature_blocks
    block_column = pattern % feature_blocks
    row_select = (block_row[:, None] == jnp.arange(row_blocks, dtype=jnp.int32)[None, :]).astype(
        jnp.float32
    )
    column_select = (
        block_column[:, None] == jnp.arange(feature_blocks, dtype=jnp.int32)[None, :]
    ).astype(jnp.float32)
    global_rows = lax.axis_index("row") * row_count + jnp.arange(row_count, dtype=jnp.int32)
    removed = jnp.any(global_rows[:, None] == deleted[None, :], axis=1)
    logistic = jax.nn.sigmoid(margins)
    weights_flat = jnp.where(removed, 0.0, logistic * (1.0 - logistic))
    weights = weights_flat.reshape(row_blocks, block_width, 1)
    share_rows = feature_rows // lax.axis_size("row")
    offset = lax.axis_index("row") * share_rows

    def own_rows(values):
        return lax.dynamic_slice_in_dim(values, offset, share_rows, 0)

    residual = grads
    solution = jnp.zeros_like(residual)
    direction = residual
    mine = own_rows(residual)
    norm_now = lax.psum(jnp.sum(mine * mine, axis=0), ("row", "col"))
    for iteration in range(ITERS):
        apply_rounded = direction.astype(jnp.bfloat16)
        picked_tiles = apply_rounded.reshape(feature_blocks, block_width, directions)[block_column]
        forward = jnp.einsum(
            "bij,bjk->bik", x_blocks, picked_tiles, preferred_element_type=jnp.float32
        )
        partial_rows = jnp.einsum("br,bik->rik", row_select, forward, precision=highest)
        projected = lax.psum(partial_rows, "col")
        scaled = (weights * projected).astype(jnp.bfloat16)
        picked_rows = scaled[block_row]
        backward = jnp.einsum(
            "bji,bjk->bik", x_blocks, picked_rows, preferred_element_type=jnp.float32
        )
        summed = jnp.einsum("bc,bik->cik", column_select, backward, precision=highest)
        hessian_image = (
            lax.psum(summed.reshape(feature_rows, directions), "row") + ridge_weight * direction
        )
        own_image = own_rows(hessian_image)
        own_residual = own_rows(residual)
        curvature, cross_term, image_square = lax.psum(
            (
                jnp.sum(own_rows(direction) * own_image, axis=0),
                jnp.sum(own_residual * own_image, axis=0),
                jnp.sum(own_image * own_image, axis=0),
            ),
            ("row", "col"),
        )
        step_size = norm_now / curvature
        norm_next = norm_now - 2.0 * step_size * cross_term + step_size * step_size * image_square
        solution = solution + step_size * direction
        residual = residual - step_size * hessian_image
        if iteration + 1 < ITERS:
            direction = residual + norm_next / norm_now * direction
            norm_now = norm_next
    return (solution, residual)


def solution(mesh):
    placed = (P("row", "col", None), P("row", "col"), P("row"), P("row"), P("col", None))
    return jax.shard_map(
        on_device,
        mesh=mesh,
        in_specs=placed,
        out_specs=(P("col", None), P("col", None)),
        check_vma=False,
    )
```

profile of v0, /device:TPU:0, one launch (start us, length us, event | category | flops | bytes accessed | tf_op | source)
XLA Modules:
  0.0 801.8 jit_solution(736054281682014846)
XLA Ops:
  7.2 0.0 all-reduce.9.cloned.1.call-start
  7.2 0.7 compare_select_fusion
  7.9 1.3 convert_element_type.20
  9.2 8.6 %gather_fusion = bf16[256,128,128]{2,1,0:T(8,128)(2,1)} fusion(bf16[16,128,128]{2,1,0:T(8,128)(2,1)S(1)} %bitcast.54, s32[1024]{0:T(1024)S(1)} %pad_clamp_fusion.1), kind=kCustom, calls=%fused_computation | custom fusion | bytes 16778240 | tf_op jit(solution)/shard_map/gather | solution.py:45
  17.8 12.8 %convolution_bitcast_fusion.5 = f32[256,128,128]{1,2,0:T(8,128)} fusion(bf16[256,128,128]{2,1,0:T(8,128)(2,1)} %gather_fusion, bf16[256,128,128]{2,1,0:T(8,128)(2,1)} %param.5), kind=kOutput, calls=%fused_computation.11 | convolution fusion | flops 1073741824 | bytes 33554432 | tf_op jit(solution)/shard_map/bij,bjk->bik/dot_general | solution.py:46
  30.6 17.5 %copy.24 = f32[256,128,128]{2,0,1:T(8,128)} copy(f32[256,128,128]{1,2,0:T(8,128)} %convolution_bitcast_fusion.5) | data formatting | bytes 33554432 | tf_op jit(solution)/shard_map/bij,bjk->bik/dot_general | solution.py:46
  48.1 10.8 %fusion.5 = f32[32,128,128]{2,0,1:T(8,128)} fusion(f32[256,128,128]{2,0,1:T(8,128)} %copy.24, s32[256]{0:T(256)S(1)} %bitcast.61), kind=kOutput, calls=%fused_computation.36 | convolution fusion | flops 1610620928 | bytes 18875392 | tf_op jit(solution)/shard_map/br,bik->rik/dot_general | solution.py:49
  58.9 0.0 all-reduce.9.cloned.1.call-update
  58.9 0.3 all-reduce.11.cloned.1.call-start
  59.2 1.5 compare_reduce_fusion
  60.8 0.1 copy.22
  60.9 62.7 %all-reduce.9.cloned.1.call-done = f32[32,128,128]{2,0,1:T(8,128)} async-done(((f32[32,128,128]{2,0,1:T(8,128)}), f32[32,128,128]{2,0,1:T(8,128)}) %all-reduce.9.cloned.1.call-update) | async-done | bytes 2097168 | tf_op jit(solution)/shard_map/psum | solution.py:50
  123.6 1.9 multiply_convert_fusion.2
  125.5 0.4 copy.25
  125.9 8.6 %gather_fusion.1 = bf16[256,128,128]{2,1,0:T(8,128)(2,1)} fusion(bf16[32,128,128]{2,1,0:T(8,128)(2,1)S(1)} %copy.25, s32[1024]{0:T(1024)S(1)} %pad_clamp_fusion), kind=kCustom, calls=%fused_computation.1 | custom fusion | bytes 16778240 | tf_op jit(solution)/shard_map/gather | solution.py:52
  134.5 14.4 %convolution_bitcast_fusion.4 = f32[256,128,128]{1,2,0:T(8,128)} fusion(bf16[256,128,128]{2,1,0:T(8,128)(2,1)} %gather_fusion.1, bf16[256,128,128]{2,1,0:T(8,128)(2,1)} %param.5), kind=kOutput, calls=%fused_computation.10 | convolution fusion | flops 1073741824 | bytes 33554432 | tf_op jit(solution)/shard_map/bji,bjk->bik/dot_general | solution.py:53
  148.9 17.5 %copy.27 = f32[256,128,128]{2,0,1:T(8,128)} copy(f32[256,128,128]{1,2,0:T(8,128)} %convolution_bitcast_fusion.4) | data formatting | bytes 33554432 | tf_op jit(solution)/shard_map/bji,bjk->bik/dot_general | solution.py:53
  166.4 9.1 %fusion.17 = f32[16,128,128]{2,0,1:T(8,128)S(1)} fusion(f32[256,128,128]{2,0,1:T(8,128)} %copy.27, s32[256]{0:T(256)S(1)} %bitcast.58), kind=kOutput, calls=%fused_computation.48 | convolution fusion | flops 805310464 | bytes 17826816 | tf_op jit(solution)/shard_map/bc,bik->cik/dot_general | solution.py:56
  175.5 1.3 copy.28
  176.8 0.0 all-reduce.13.cloned.1.call-start
  176.9 51.1 %all-reduce.11.cloned.1.call-done = f32[2048,128]{1,0:T(8,128)} async-done(((f32[2048,128]{1,0:T(8,128)}), f32[2048,128]{1,0:T(8,128)}) %all-reduce.11.cloned.1.call-update) | async-done | bytes 1048592 | tf_op jit(solution)/shard_map/psum | solution.py:58
  228.0 1.3 multiply_add_fusion.5
  229.3 0.1 multiply_reduce_fusion.4
  229.4 40.4 %all-reduce.1 = (f32[128]{0:T(128)S(1)}, f32[128]{0:T(128)S(1)}, f32[128]{0:T(128)S(1)}) all-reduce(f32[128]{0:T(128)S(1)} %get-tuple-element.7, f32[128]{0:T(128)S(1)} %get-tuple-element.6, f32[128]{0:T(128)S(1)} %get-tuple-element.5), channel_id=1, replica_groups=mesh['row'=4,'col'=8] {'row','col'}, use_global_device_ids=true, to_apply=%region_1.2 | all-reduce | flops 384 | bytes 3072 | tf_op jit(solution)/shard_map/psum | solution.py:42
  269.8 2.4 fusion.24
  272.3 8.6 %gather_fusion.2 = bf16[256,128,128]{2,1,0:T(8,128)(2,1)} fusion(bf16[16,128,128]{2,1,0:T(8,128)(2,1)S(1)} %bitcast.52, s32[1024]{0:T(1024)S(1)} %pad_clamp_fusion.1), kind=kCustom, calls=%fused_computation.2 | custom fusion | bytes 16778240 | tf_op jit(solution)/shard_map/gather | solution.py:45
  280.8 12.8 %convolution_bitcast_fusion.3 = f32[256,128,128]{1,2,0:T(8,128)} fusion(bf16[256,128,128]{2,1,0:T(8,128)(2,1)} %gather_fusion.2, bf16[256,128,128]{2,1,0:T(8,128)(2,1)} %param.5), kind=kOutput, calls=%fused_computation.9 | convolution fusion | flops 1073741824 | bytes 33554432 | tf_op jit(solution)/shard_map/bij,bjk->bik/dot_general | solution.py:46
  293.7 17.5 %copy.30 = f32[256,128,128]{2,0,1:T(8,128)} copy(f32[256,128,128]{1,2,0:T(8,128)} %convolution_bitcast_fusion.3) | data formatting | bytes 33554432 | tf_op jit(solution)/shard_map/bij,bjk->bik/dot_general | solution.py:46
  311.2 10.7 %fusion.3 = f32[32,128,128]{2,0,1:T(8,128)} fusion(f32[256,128,128]{2,0,1:T(8,128)} %copy.30, s32[256]{0:T(256)S(1)} %bitcast.62), kind=kOutput, calls=%fused_computation.35 | convolution fusion | flops 1610620928 | bytes 18875392 | tf_op jit(solution)/shard_map/br,bik->rik/dot_general | solution.py:49
  321.9 0.0 all-reduce.13.cloned.1.call-update
  321.9 0.2 all-reduce.15.cloned.1.call-start
  322.1 61.1 %all-reduce.13.cloned.1.call-done = f32[32,128,128]{2,0,1:T(8,128)} async-done(((f32[32,128,128]{2,0,1:T(8,128)}), f32[32,128,128]{2,0,1:T(8,128)}) %all-reduce.13.cloned.1.call-update) | async-done | bytes 2097168 | tf_op jit(solution)/shard_map/psum | solution.py:50
  383.2 1.9 multiply_convert_fusion.1
  385.2 0.4 copy.31
  385.6 8.6 %gather_fusion.3 = bf16[256,128,128]{2,1,0:T(8,128)(2,1)} fusion(bf16[32,128,128]{2,1,0:T(8,128)(2,1)S(1)} %copy.31, s32[1024]{0:T(1024)S(1)} %pad_clamp_fusion), kind=kCustom, calls=%fused_computation.3 | custom fusion | bytes 16778240 | tf_op jit(solution)/shard_map/gather | solution.py:52
  394.2 14.4 %convolution_bitcast_fusion.2 = f32[256,128,128]{1,2,0:T(8,128)} fusion(bf16[256,128,128]{2,1,0:T(8,128)(2,1)} %gather_fusion.3, bf16[256,128,128]{2,1,0:T(8,128)(2,1)} %param.5), kind=kOutput, calls=%fused_computation.8 | convolution fusion | flops 1073741824 | bytes 33554432 | tf_op jit(solution)/shard_map/bji,bjk->bik/dot_general | solution.py:53
  408.6 17.5 %copy.33 = f32[256,128,128]{2,0,1:T(8,128)} copy(f32[256,128,128]{1,2,0:T(8,128)} %convolution_bitcast_fusion.2) | data formatting | bytes 33554432 | tf_op jit(solution)/shard_map/bji,bjk->bik/dot_general | solution.py:53
  426.0 9.0 %fusion.15 = f32[16,128,128]{2,0,1:T(8,128)S(1)} fusion(f32[256,128,128]{2,0,1:T(8,128)} %copy.33, s32[256]{0:T(256)S(1)} %bitcast.59), kind=kOutput, calls=%fused_computation.47 | convolution fusion | flops 805310464 | bytes 17826816 | tf_op jit(solution)/shard_map/bc,bik->cik/dot_general | solution.py:56
  435.1 1.3 copy.34
  436.4 0.0 all-reduce.15.cloned.1.call-update
  436.4 0.0 all-reduce.17.cloned.1.call-start
  436.5 51.1 %all-reduce.15.cloned.1.call-done = f32[2048,128]{1,0:T(8,128)} async-done(((f32[2048,128]{1,0:T(8,128)}), f32[2048,128]{1,0:T(8,128)}) %all-reduce.15.cloned.1.call-update) | async-done | bytes 1048592 | tf_op jit(solution)/shard_map/psum | solution.py:58
  487.5 1.3 multiply_add_fusion.3
  488.9 1.0 multiply_reduce_fusion.2
  489.9 40.2 %all-reduce = (f32[128]{0:T(128)S(1)}, f32[128]{0:T(128)S(1)}, f32[128]{0:T(128)S(1)}) all-reduce(f32[128]{0:T(128)S(1)} %get-tuple-element.3, f32[128]{0:T(128)S(1)} %get-tuple-element.4, f32[128]{0:T(128)S(1)} %get-tuple-element.2), channel_id=1, replica_groups=mesh['row'=4,'col'=8] {'row','col'}, use_global_device_ids=true, to_apply=%region_16.17 | all-reduce | flops 384 | bytes 3072 | tf_op jit(solution)/shard_map/psum | solution.py:62
  530.1 2.8 fusion.22
  532.9 8.6 %gather_fusion.4 = bf16[256,128,128]{2,1,0:T(8,128)(2,1)} fusion(bf16[16,128,128]{2,1,0:T(8,128)(2,1)S(1)} %bitcast.53, s32[1024]{0:T(1024)S(1)} %pad_clamp_fusion.1), kind=kCustom, calls=%fused_computation.4 | custom fusion | bytes 16778240 | tf_op jit(solution)/shard_map/gather | solution.py:45
  541.5 12.8 %convolution_bitcast_fusion.1 = f32[256,128,128]{1,2,0:T(8,128)} fusion(bf16[256,128,128]{2,1,0:T(8,128)(2,1)} %gather_fusion.4, bf16[256,128,128]{2,1,0:T(8,128)(2,1)} %param.5), kind=kOutput, calls=%fused_computation.7 | convolution fusion | flops 1073741824 | bytes 33554432 | tf_op jit(solution)/shard_map/bij,bjk->bik/dot_general | solution.py:46
  554.3 17.5 %copy.36 = f32[256,128,128]{2,0,1:T(8,128)} copy(f32[256,128,128]{1,2,0:T(8,128)} %convolution_bitcast_fusion.1) | data formatting | bytes 33554432 | tf_op jit(solution)/shard_map/bij,bjk->bik/dot_general | solution.py:46
  571.8 10.7 %fusion.1 = f32[32,128,128]{2,0,1:T(8,128)} fusion(f32[256,128,128]{2,0,1:T(8,128)} %copy.36, s32[256]{0:T(256)S(1)} %bitcast.63), kind=kOutput, calls=%fused_computation.34 | convolution fusion | flops 1610620928 | bytes 18875392 | tf_op jit(solution)/shard_map/br,bik->rik/dot_general | solution.py:49
  582.6 0.3 all-reduce.19.cloned.1.call-start
  582.9 60.9 %all-reduce.17.cloned.1.call-done = f32[32,128,128]{2,0,1:T(8,128)} async-done(((f32[32,128,128]{2,0,1:T(8,128)}), f32[32,128,128]{2,0,1:T(8,128)}) %all-reduce.17.cloned.1.call-update) | async-done | bytes 2097168 | tf_op jit(solution)/shard_map/psum | solution.py:50
  643.8 1.9 multiply_convert_fusion
  645.7 0.4 copy.37
  646.2 8.6 %gather_fusion.5 = bf16[256,128,128]{2,1,0:T(8,128)(2,1)} fusion(bf16[32,128,128]{2,1,0:T(8,128)(2,1)S(1)} %copy.37, s32[1024]{0:T(1024)S(1)} %pad_clamp_fusion), kind=kCustom, calls=%fused_computation.5 | custom fusion | bytes 16778240 | tf_op jit(solution)/shard_map/gather | solution.py:52
  654.8 14.4 %convolution_bitcast_fusion = f32[256,128,128]{1,2,0:T(8,128)} fusion(bf16[256,128,128]{2,1,0:T(8,128)(2,1)} %gather_fusion.5, bf16[256,128,128]{2,1,0:T(8,128)(2,1)} %param.5), kind=kOutput, calls=%fused_computation.6 | convolution fusion | flops 1073741824 | bytes 33554432 | tf_op jit(solution)/shard_map/bji,bjk->bik/dot_general | solution.py:53
  669.1 17.5 %copy.39 = f32[256,128,128]{2,0,1:T(8,128)} copy(f32[256,128,128]{1,2,0:T(8,128)} %convolution_bitcast_fusion) | data formatting | bytes 33554432 | tf_op jit(solution)/shard_map/bji,bjk->bik/dot_general | solution.py:53
  686.6 9.1 %fusion.13 = f32[16,128,128]{2,0,1:T(8,128)S(1)} fusion(f32[256,128,128]{2,0,1:T(8,128)} %copy.39, s32[256]{0:T(256)S(1)} %bitcast.60), kind=kOutput, calls=%fused_computation.46 | convolution fusion | flops 805310464 | bytes 17826816 | tf_op jit(solution)/shard_map/bc,bik->cik/dot_general | solution.py:56
  695.8 1.4 copy.40
  697.1 51.1 %all-reduce.19.cloned.1.call-done = f32[2048,128]{1,0:T(8,128)} async-done(((f32[2048,128]{1,0:T(8,128)}), f32[2048,128]{1,0:T(8,128)}) %all-reduce.19.cloned.1.call-update) | async-done | bytes 1048592 | tf_op jit(solution)/shard_map/psum | solution.py:58
  748.3 1.7 multiply_add_fusion.1
  749.9 1.0 multiply_reduce_fusion
  751.0 40.0 %psum.106 = f32[128]{0:T(128)S(1)} all-reduce(f32[128]{0:T(128)S(1)} %multiply_reduce_fusion), channel_id=1, replica_groups=mesh['row'=4,'col'=8] {'row','col'}, use_global_device_ids=true, to_apply=%region_20.21 | all-reduce | flops 128 | bytes 1024 | tf_op jit(solution)/shard_map/psum | solution.py:62
  790.9 3.6 multiply_subtract_fusion
  (19 shorter events, 0.1 us)
Async XLA Ops:
  7.2 116.4 %all-reduce.9.cloned.1.call-start = ((), (), s32[]{:S(2)}) async-start(), calls=%async_computation | async-start | bytes 4194304 | tf_op jit(solution)/shard_map/psum | solution.py:50
  48.1 11.1 %copy-start.3 = (s32[512]{0:T(512)S(1)}, s32[512]{0:T(512)}, u32[]{:S(2)}) copy-start(s32[512]{0:T(512)} %param.8) | copy-start | bytes 6148
  48.1 12.6 %copy-start.2 = (f32[4096]{0:T(1024)S(1)}, f32[4096]{0:T(1024)}, u32[]{:S(2)}) copy-start(f32[4096]{0:T(1024)} %param.7) | copy-start | bytes 49156
  58.9 169.0 %all-reduce.11.cloned.1.call-start = ((), (), s32[]{:S(2)}) async-start(), calls=%async_computation.1 | async-start | bytes 2097152 | tf_op jit(solution)/shard_map/psum | solution.py:58
  166.4 61.6 %copy-start = (f32[2048,128]{1,0:T(8,128)S(1)}, f32[2048,128]{1,0:T(8,128)}, u32[]{:S(2)}) copy-start(f32[2048,128]{1,0:T(8,128)} %param.9) | copy-start | bytes 3145732
  176.8 206.4 %all-reduce.13.cloned.1.call-start = ((), (), s32[]{:S(2)}) async-start(), calls=%async_computation.2 | async-start | bytes 4194304 | tf_op jit(solution)/shard_map/psum | solution.py:50
  321.9 165.6 %all-reduce.15.cloned.1.call-start = ((), (), s32[]{:S(2)}) async-start(), calls=%async_computation.3 | async-start | bytes 2097152 | tf_op jit(solution)/shard_map/psum | solution.py:58
  436.4 207.4 %all-reduce.17.cloned.1.call-start = ((), (), s32[]{:S(2)}) async-start(), calls=%async_computation.4 | async-start | bytes 4194304 | tf_op jit(solution)/shard_map/psum | solution.py:50
  582.6 165.7 %all-reduce.19.cloned.1.call-start = ((), (), s32[]{:S(2)}) async-start(), calls=%async_computation.5 | async-start | bytes 2097152 | tf_op jit(solution)/shard_map/psum | solution.py:58
  686.6 104.3 %copy-start.1 = (f32[2048,128]{1,0:T(8,128)S(1)}, f32[2048,128]{1,0:T(8,128)}, u32[]{:S(2)}) copy-start(f32[2048,128]{1,0:T(8,128)} %get-tuple-element.21) | copy-start | bytes 3145732
Sparse Core Ops, SparseCore 0:
  59.0 64.4 all-reduce.8
  177.0 50.9 all-reduce.10
  322.0 61.1 all-reduce.12
  436.5 50.9 all-reduce.14
  582.7 61.0 all-reduce.16
  697.3 50.9 all-reduce.18
where the time goes:
time: 810 us; the launch traced here: 802 us
  waiting for transfers between devices  338 us (42%)
  local copies, waits for them, and re-layouts  162 us (20%)
  matrix products  141 us (17%)
  blocking collectives  121 us (15%)
  other arithmetic  24.7 us (3%)
  between operations  14.7 us (2%)
    psum x3, waiting for transfers between devices, on_device(): projected = lax.psum(partial_rows, 'col')  185 us
    psum x3, waiting for transfers between devices, on_device(): lax.psum(summed.reshape(feature_rows, directions), 'row')  153 us
    psum x2, blocking collectives, on_device(): lax.psum((jnp.sum(own_rows(direction) * own_image, axis=0), jnp.sum(own_r...  80.2 us
    dot_general x3, local copies, waits for them, and re-layouts, on_device(): jnp.einsum('bij,bjk->bik', x_blocks, picked_tiles, preferred_element_type...  52.4 us
    dot_general x3, local copies, waits for them, and re-layouts, on_device(): jnp.einsum('bji,bjk->bik', x_blocks, picked_rows, preferred_element_type=...  52.4 us
    dot_general x3, matrix products, on_device(): jnp.einsum('bji,bjk->bik', x_blocks, picked_rows, preferred_element_type=...  43.1 us
    psum x1, blocking collectives, on_device(): norm_now = lax.psum(jnp.sum(mine * mine, axis=0), ('row', 'col'))  40.4 us
    dot_general x3, matrix products, on_device(): jnp.einsum('bij,bjk->bik', x_blocks, picked_tiles, preferred_element_type...  38.5 us
  transfers between devices with their start and end apart: 6, of which 6 were waited for; matrix products, arithmetic and copies ran while one was open for 0% of the time, Pallas kernels for 0%

commit v1 on v0

--- a/solution.py
+++ b/solution.py
@@ -47,7 +47,10 @@
             "bij,bjk->bik", x_blocks, picked_tiles, preferred_element_type=jnp.float32
         )
         partial_rows = jnp.einsum("br,bik->rik", row_select, forward, precision=highest)
-        projected = lax.psum(partial_rows, "col")
+        devices, projected = (lax.axis_size("col"), partial_rows)
+        for far in [1 << k for k in range(devices.bit_length() - 1)]:
+            swap = [(i, i ^ far) for i in range(devices)]
+            projected = projected + lax.ppermute(projected, "col", swap)
         scaled = (weights * projected).astype(jnp.bfloat16)
         picked_rows = scaled[block_row]
         backward = jnp.einsum(

time: 810 us -> 923 us (1.14)
  waiting for transfers between devices: 338 us -> 439 us
  starting transfers between devices: 0.88 us -> 13.9 us
    ppermute x0 -> x9, waiting for transfers between devices: none -> 284 us  [on_device(): projected = projected + lax.ppermute(projected, 'col', swap)]
    psum x3 -> x0, waiting for transfers between devices: 185 us -> none  [on_device(): projected = lax.psum(partial_rows, 'col')]
    ppermute x0 -> x9, starting transfers between devices: none -> 13.7 us  [on_device(): projected = projected + lax.ppermute(projected, 'col', swap)]
  transfers between devices with their start and end apart: 6 -> 12, of which waited for: 6 -> 12; matrix products, arithmetic and copies ran while one was open for 0% -> 0% of each run, Pallas kernels for 0% -> 0%
where the time goes in v1:
time: 923 us; the launch traced here: 913 us
  waiting for transfers between devices  439 us (48%)
  local copies, waits for them, and re-layouts  162 us (18%)
  matrix products  138 us (15%)
  blocking collectives  121 us (13%)
  other arithmetic  25.2 us (3%)
  between operations  14.4 us (2%)
  starting transfers between devices  13.9 us (2%)
    ppermute x9, waiting for transfers between devices, on_device(): projected = projected + lax.ppermute(projected, 'col', swap)  284 us
    psum x3, waiting for transfers between devices, on_device(): lax.psum(summed.reshape(feature_rows, directions), 'row')  154 us
    psum x2, blocking collectives, on_device(): lax.psum((jnp.sum(own_rows(direction) * own_image, axis=0), jnp.sum(own_r...  80.2 us
    dot_general x3, local copies, waits for them, and re-layouts, on_device(): jnp.einsum('bij,bjk->bik', x_blocks, picked_tiles, preferred_element_type...  52.4 us
    dot_general x3, local copies, waits for them, and re-layouts, on_device(): jnp.einsum('bji,bjk->bik', x_blocks, picked_rows, preferred_element_type=...  52.4 us
    dot_general x3, matrix products, on_device(): jnp.einsum('bji,bjk->bik', x_blocks, picked_rows, preferred_element_type=...  43.1 us
    psum x1, blocking collectives, on_device(): norm_now = lax.psum(jnp.sum(mine * mine, axis=0), ('row', 'col'))  40.4 us
    dot_general x3, matrix products, on_device(): jnp.einsum('bij,bjk->bik', x_blocks, picked_tiles, preferred_element_type...  38.5 us
  transfers between devices with their start and end apart: 12, of which 12 were waited for; matrix products, arithmetic and copies ran while one was open for 0% of the time, Pallas kernels for 0%

profile of v1, /device:TPU:0, one launch (start us, length us, event | category | flops | bytes accessed | tf_op | source)
XLA Modules:
  0.0 913.3 jit_solution(5008541524430395979)
XLA Ops:
  7.2 0.7 compare_select_fusion
  7.9 1.3 convert_element_type.20
  9.2 8.6 gather_fusion
  17.8 12.8 %convolution_bitcast_fusion.5 = f32[256,128,128]{1,2,0:T(8,128)} fusion(bf16[256,128,128]{2,1,0:T(8,128)(2,1)} %gather_fusion, bf16[256,128,128]{2,1,0:T(8,128)(2,1)} %param.5), kind=kOutput, calls=%fused_computation.11 | convolution fusion | flops 1073741824 | bytes 33554432 | tf_op jit(solution)/shard_map/bij,bjk->bik/dot_general | solution.py:46
  30.6 17.5 %copy.32 = f32[256,128,128]{2,0,1:T(8,128)} copy(f32[256,128,128]{1,2,0:T(8,128)} %convolution_bitcast_fusion.5) | data formatting | bytes 33554432 | tf_op jit(solution)/shard_map/bij,bjk->bik/dot_general | solution.py:46
  48.1 9.8 %fusion.5 = f32[32,128,128]{2,0,1:T(8,128)S(1)} fusion(f32[256,128,128]{2,0,1:T(8,128)} %copy.32, s32[256]{0:T(256)S(1)} %bitcast.61), kind=kOutput, calls=%fused_computation.36 | convolution fusion | flops 1610620928 | bytes 18875392 | tf_op jit(solution)/shard_map/br,bik->rik/dot_general | solution.py:49
  57.9 0.6 collective-permute-start
  58.5 3.8 collective-permute-done
  62.3 0.5 add.128
  62.7 2.9 collective-permute-start.1
  65.6 45.9 %collective-permute-done.1 = f32[32,128,128]{2,0,1:T(8,128)S(1)} collective-permute-done((f32[32,128,128]{2,0,1:T(8,128)S(1)}, f32[32,128,128]{2,0,1:T(8,128)S(1)}, u32[]{:S(2)}, u32[]{:S(2)}) %collective-permute-start.1) | collective-permute-done | bytes 2097184 | tf_op jit(solution)/shard_map/ppermute | solution.py:53
  112.1 1.8 collective-permute-start.2
  113.9 1.5 compare_reduce_fusion
  115.6 43.7 %collective-permute-done.2 = f32[32,128,128]{2,0,1:T(8,128)} collective-permute-done((f32[32,128,128]{2,0,1:T(8,128)S(1)}, f32[32,128,128]{2,0,1:T(8,128)}, u32[]{:S(2)}, u32[]{:S(2)}) %collective-permute-start.2) | collective-permute-done | bytes 2097184 | tf_op jit(solution)/shard_map/ppermute | solution.py:53
  159.3 1.9 multiply_convert_fusion.2
  161.7 8.8 gather_fusion.1
  170.5 14.4 %convolution_bitcast_fusion.4 = f32[256,128,128]{1,2,0:T(8,128)} fusion(bf16[256,128,128]{2,1,0:T(8,128)(2,1)} %gather_fusion.1, bf16[256,128,128]{2,1,0:T(8,128)(2,1)} %param.5), kind=kOutput, calls=%fused_computation.10 | convolution fusion | flops 1073741824 | bytes 33554432 | tf_op jit(solution)/shard_map/bji,bjk->bik/dot_general | solution.py:56
  184.9 17.5 %copy.35 = f32[256,128,128]{2,0,1:T(8,128)} copy(f32[256,128,128]{1,2,0:T(8,128)} %convolution_bitcast_fusion.4) | data formatting | bytes 33554432 | tf_op jit(solution)/shard_map/bji,bjk->bik/dot_general | solution.py:56
  202.4 9.1 fusion.17
  211.5 1.3 copy.36
  212.9 53.2 %all-reduce.6.cloned.1.call-done = f32[2048,128]{1,0:T(8,128)} async-done(((f32[2048,128]{1,0:T(8,128)}), f32[2048,128]{1,0:T(8,128)}) %all-reduce.6.cloned.1.call-update) | async-done | bytes 1048592 | tf_op jit(solution)/shard_map/psum | solution.py:61
  266.1 1.3 multiply_add_fusion.5
  267.5 40.4 %all-reduce.1 = (f32[128]{0:T(128)S(1)}, f32[128]{0:T(128)S(1)}, f32[128]{0:T(128)S(1)}) all-reduce(f32[128]{0:T(128)S(1)} %get-tuple-element.7, f32[128]{0:T(128)S(1)} %get-tuple-element.6, f32[128]{0:T(128)S(1)} %get-tuple-element.5), channel_id=1, replica_groups=mesh['row'=4,'col'=8] {'row','col'}, use_global_device_ids=true, to_apply=%region_1.2 | all-reduce | flops 384 | bytes 3072 | tf_op jit(solution)/shard_map/psum | solution.py:42
  307.9 2.4 fusion.24
  310.4 8.6 gather_fusion.2
  319.0 12.8 %convolution_bitcast_fusion.3 = f32[256,128,128]{1,2,0:T(8,128)} fusion(bf16[256,128,128]{2,1,0:T(8,128)(2,1)} %gather_fusion.2, bf16[256,128,128]{2,1,0:T(8,128)(2,1)} %param.5), kind=kOutput, calls=%fused_computation.9 | convolution fusion | flops 1073741824 | bytes 33554432 | tf_op jit(solution)/shard_map/bij,bjk->bik/dot_general | solution.py:46
  331.8 17.5 %copy.38 = f32[256,128,128]{2,0,1:T(8,128)} copy(f32[256,128,128]{1,2,0:T(8,128)} %convolution_bitcast_fusion.3) | data formatting | bytes 33554432 | tf_op jit(solution)/shard_map/bij,bjk->bik/dot_general | solution.py:46
  349.3 9.7 %fusion.3 = f32[32,128,128]{2,0,1:T(8,128)S(1)} fusion(f32[256,128,128]{2,0,1:T(8,128)} %copy.38, s32[256]{0:T(256)S(1)} %bitcast.62), kind=kOutput, calls=%fused_computation.35 | convolution fusion | flops 1610620928 | bytes 18875392 | tf_op jit(solution)/shard_map/br,bik->rik/dot_general | solution.py:49
  359.1 4.1 collective-permute-done.3
  363.8 2.3 collective-permute-start.4
  366.1 45.9 %collective-permute-done.4 = f32[32,128,128]{2,0,1:T(8,128)S(1)} collective-permute-done((f32[32,128,128]{2,0,1:T(8,128)S(1)}, f32[32,128,128]{2,0,1:T(8,128)S(1)}, u32[]{:S(2)}, u32[]{:S(2)}) %collective-permute-start.4) | collective-permute-done | bytes 2097184 | tf_op jit(solution)/shard_map/ppermute | solution.py:53
  412.5 1.8 collective-permute-start.5
  414.3 45.4 %collective-permute-done.5 = f32[32,128,128]{2,0,1:T(8,128)S(1)} collective-permute-done((f32[32,128,128]{2,0,1:T(8,128)S(1)}, f32[32,128,128]{2,0,1:T(8,128)S(1)}, u32[]{:S(2)}, u32[]{:S(2)}) %collective-permute-start.5) | collective-permute-done | bytes 2097184 | tf_op jit(solution)/shard_map/ppermute | solution.py:53
  459.7 0.7 multiply_convert_fusion.1
  460.8 8.8 gather_fusion.3
  469.6 14.4 %convolution_bitcast_fusion.2 = f32[256,128,128]{1,2,0:T(8,128)} fusion(bf16[256,128,128]{2,1,0:T(8,128)(2,1)} %gather_fusion.3, bf16[256,128,128]{2,1,0:T(8,128)(2,1)} %param.5), kind=kOutput, calls=%fused_computation.8 | convolution fusion | flops 1073741824 | bytes 33554432 | tf_op jit(solution)/shard_map/bji,bjk->bik/dot_general | solution.py:56
  484.0 17.5 %copy.41 = f32[256,128,128]{2,0,1:T(8,128)} copy(f32[256,128,128]{1,2,0:T(8,128)} %convolution_bitcast_fusion.2) | data formatting | bytes 33554432 | tf_op jit(solution)/shard_map/bji,bjk->bik/dot_general | solution.py:56
  501.5 9.0 fusion.15
  510.5 1.3 copy.42
  511.9 50.5 %all-reduce.8.cloned.1.call-done = f32[2048,128]{1,0:T(8,128)} async-done(((f32[2048,128]{1,0:T(8,128)}), f32[2048,128]{1,0:T(8,128)}) %all-reduce.8.cloned.1.call-update) | async-done | bytes 1048592 | tf_op jit(solution)/shard_map/psum | solution.py:61
  562.4 1.3 multiply_add_fusion.3
  563.8 1.0 multiply_reduce_fusion.2
  564.8 40.2 %all-reduce = (f32[128]{0:T(128)S(1)}, f32[128]{0:T(128)S(1)}, f32[128]{0:T(128)S(1)}) all-reduce(f32[128]{0:T(128)S(1)} %get-tuple-element.3, f32[128]{0:T(128)S(1)} %get-tuple-element.4, f32[128]{0:T(128)S(1)} %get-tuple-element.2), channel_id=1, replica_groups=mesh['row'=4,'col'=8] {'row','col'}, use_global_device_ids=true, to_apply=%region_14.15 | all-reduce | flops 384 | bytes 3072 | tf_op jit(solution)/shard_map/psum | solution.py:65
  605.0 2.8 fusion.22
  607.8 8.6 gather_fusion.4
  616.4 12.8 %convolution_bitcast_fusion.1 = f32[256,128,128]{1,2,0:T(8,128)} fusion(bf16[256,128,128]{2,1,0:T(8,128)(2,1)} %gather_fusion.4, bf16[256,128,128]{2,1,0:T(8,128)(2,1)} %param.5), kind=kOutput, calls=%fused_computation.7 | convolution fusion | flops 1073741824 | bytes 33554432 | tf_op jit(solution)/shard_map/bij,bjk->bik/dot_general | solution.py:46
  629.2 17.5 %copy.44 = f32[256,128,128]{2,0,1:T(8,128)} copy(f32[256,128,128]{1,2,0:T(8,128)} %convolution_bitcast_fusion.1) | data formatting | bytes 33554432 | tf_op jit(solution)/shard_map/bij,bjk->bik/dot_general | solution.py:46
  646.7 9.7 %fusion.1 = f32[32,128,128]{2,0,1:T(8,128)S(1)} fusion(f32[256,128,128]{2,0,1:T(8,128)} %copy.44, s32[256]{0:T(256)S(1)} %bitcast.63), kind=kOutput, calls=%fused_computation.34 | convolution fusion | flops 1610620928 | bytes 18875392 | tf_op jit(solution)/shard_map/br,bik->rik/dot_general | solution.py:49
  656.5 4.1 collective-permute-done.6
  661.1 2.3 collective-permute-start.7
  663.5 45.9 %collective-permute-done.7 = f32[32,128,128]{2,0,1:T(8,128)S(1)} collective-permute-done((f32[32,128,128]{2,0,1:T(8,128)S(1)}, f32[32,128,128]{2,0,1:T(8,128)S(1)}, u32[]{:S(2)}, u32[]{:S(2)}) %collective-permute-start.7) | collective-permute-done | bytes 2097184 | tf_op jit(solution)/shard_map/ppermute | solution.py:53
  709.9 1.8 collective-permute-start.8
  711.7 45.4 %collective-permute-done.8 = f32[32,128,128]{2,0,1:T(8,128)S(1)} collective-permute-done((f32[32,128,128]{2,0,1:T(8,128)S(1)}, f32[32,128,128]{2,0,1:T(8,128)S(1)}, u32[]{:S(2)}, u32[]{:S(2)}) %collective-permute-start.8) | collective-permute-done | bytes 2097184 | tf_op jit(solution)/shard_map/ppermute | solution.py:53
  757.1 0.7 multiply_convert_fusion
  758.2 8.9 gather_fusion.5
  767.1 14.4 %convolution_bitcast_fusion = f32[256,128,128]{1,2,0:T(8,128)} fusion(bf16[256,128,128]{2,1,0:T(8,128)(2,1)} %gather_fusion.5, bf16[256,128,128]{2,1,0:T(8,128)(2,1)} %param.5), kind=kOutput, calls=%fused_computation.6 | convolution fusion | flops 1073741824 | bytes 33554432 | tf_op jit(solution)/shard_map/bji,bjk->bik/dot_general | solution.py:56
  781.5 17.5 %copy.47 = f32[256,128,128]{2,0,1:T(8,128)} copy(f32[256,128,128]{1,2,0:T(8,128)} %convolution_bitcast_fusion) | data formatting | bytes 33554432 | tf_op jit(solution)/shard_map/bji,bjk->bik/dot_general | solution.py:56
  798.9 9.1 fusion.13
  808.1 1.4 copy.48
  809.4 50.6 %all-reduce.10.cloned.1.call-done = f32[2048,128]{1,0:T(8,128)} async-done(((f32[2048,128]{1,0:T(8,128)}), f32[2048,128]{1,0:T(8,128)}) %all-reduce.10.cloned.1.call-update) | async-done | bytes 1048592 | tf_op jit(solution)/shard_map/psum | solution.py:61
  860.0 1.7 multiply_add_fusion.1
  861.7 1.0 multiply_reduce_fusion
  862.7 40.0 %psum.82 = f32[128]{0:T(128)S(1)} all-reduce(f32[128]{0:T(128)S(1)} %multiply_reduce_fusion), channel_id=1, replica_groups=mesh['row'=4,'col'=8] {'row','col'}, use_global_device_ids=true, to_apply=%region_17.18 | all-reduce | flops 128 | bytes 1024 | tf_op jit(solution)/shard_map/psum | solution.py:65
  902.7 3.6 multiply_subtract_fusion
  (34 shorter events, 4.2 us)
Async XLA Ops:
  7.2 258.9 %all-reduce.6.cloned.1.call-start = ((), (), s32[]{:S(2)}) async-start(), calls=%async_computation | async-start | bytes 2097152 | tf_op jit(solution)/shard_map/psum | solution.py:61
  57.9 56.0 %copy-start.3 = (s32[512]{0:T(512)S(1)}, s32[512]{0:T(512)}, u32[]{:S(2)}) copy-start(s32[512]{0:T(512)} %param.8) | copy-start | bytes 6148
  57.9 57.5 %copy-start.2 = (f32[4096]{0:T(1024)S(1)}, f32[4096]{0:T(1024)}, u32[]{:S(2)}) copy-start(f32[4096]{0:T(1024)} %param.7) | copy-start | bytes 49156
  57.9 4.4 collective-permute-start
  62.7 48.8 %collective-permute-start.1 = (f32[32,128,128]{2,0,1:T(8,128)S(1)}, f32[32,128,128]{2,0,1:T(8,128)S(1)}, u32[]{:S(2)}, u32[]{:S(2)}) collective-permute-start(f32[32,128,128]{2,0,1:T(8,128)S(1)} %add.128), channel_id=1, source_target_pairs={{0,2},{1,3},{2,0},{3,1},{4,6},{5,7},{6,4},{7,5},{8,10},{9,11},{10,... | collective-permute-start | bytes 6291464 | tf_op jit(solution)/shard_map/ppermute | solution.py:53
  112.1 47.3 %collective-permute-start.2 = (f32[32,128,128]{2,0,1:T(8,128)S(1)}, f32[32,128,128]{2,0,1:T(8,128)}, u32[]{:S(2)}, u32[]{:S(2)}) collective-permute-start(f32[32,128,128]{2,0,1:T(8,128)S(1)} %add.129), channel_id=1, source_target_pairs={{0,4},{1,5},{2,6},{3,7},{4,0},{5,1},{6,2},{7,3},{8,12},{9,13},{10,... | collective-permute-start | bytes 6291464 | tf_op jit(solution)/shard_map/ppermute | solution.py:53
  202.4 63.7 %copy-start = (f32[2048,128]{1,0:T(8,128)S(1)}, f32[2048,128]{1,0:T(8,128)}, u32[]{:S(2)}) copy-start(f32[2048,128]{1,0:T(8,128)} %param.9) | copy-start | bytes 3145732
  212.8 349.6 %all-reduce.8.cloned.1.call-start = ((), (), s32[]{:S(2)}) async-start(), calls=%async_computation.1 | async-start | bytes 2097152 | tf_op jit(solution)/shard_map/psum | solution.py:61
  359.0 4.2 collective-permute-start.3
  363.8 48.3 %collective-permute-start.4 = (f32[32,128,128]{2,0,1:T(8,128)S(1)}, f32[32,128,128]{2,0,1:T(8,128)S(1)}, u32[]{:S(2)}, u32[]{:S(2)}) collective-permute-start(f32[32,128,128]{2,0,1:T(8,128)S(1)} %add.135), channel_id=1, source_target_pairs={{0,2},{1,3},{2,0},{3,1},{4,6},{5,7},{6,4},{7,5},{8,10},{9,11},{10,... | collective-permute-start | bytes 6291464 | tf_op jit(solution)/shard_map/ppermute | solution.py:53
  412.5 47.2 %collective-permute-start.5 = (f32[32,128,128]{2,0,1:T(8,128)S(1)}, f32[32,128,128]{2,0,1:T(8,128)S(1)}, u32[]{:S(2)}, u32[]{:S(2)}) collective-permute-start(f32[32,128,128]{2,0,1:T(8,128)S(1)} %add.136), channel_id=1, source_target_pairs={{0,4},{1,5},{2,6},{3,7},{4,0},{5,1},{6,2},{7,3},{8,12},{9,13},{10,... | collective-permute-start | bytes 6291464 | tf_op jit(solution)/shard_map/ppermute | solution.py:53
  511.8 348.2 %all-reduce.10.cloned.1.call-start = ((), (), s32[]{:S(2)}) async-start(), calls=%async_computation.2 | async-start | bytes 2097152 | tf_op jit(solution)/shard_map/psum | solution.py:61
  656.4 4.2 collective-permute-start.6
  661.1 48.3 %collective-permute-start.7 = (f32[32,128,128]{2,0,1:T(8,128)S(1)}, f32[32,128,128]{2,0,1:T(8,128)S(1)}, u32[]{:S(2)}, u32[]{:S(2)}) collective-permute-start(f32[32,128,128]{2,0,1:T(8,128)S(1)} %add.142), channel_id=1, source_target_pairs={{0,2},{1,3},{2,0},{3,1},{4,6},{5,7},{6,4},{7,5},{8,10},{9,11},{10,... | collective-permute-start | bytes 6291464 | tf_op jit(solution)/shard_map/ppermute | solution.py:53
  709.9 47.2 %collective-permute-start.8 = (f32[32,128,128]{2,0,1:T(8,128)S(1)}, f32[32,128,128]{2,0,1:T(8,128)S(1)}, u32[]{:S(2)}, u32[]{:S(2)}) collective-permute-start(f32[32,128,128]{2,0,1:T(8,128)S(1)} %add.143), channel_id=1, source_target_pairs={{0,4},{1,5},{2,6},{3,7},{4,0},{5,1},{6,2},{7,3},{8,12},{9,13},{10,... | collective-permute-start | bytes 6291464 | tf_op jit(solution)/shard_map/ppermute | solution.py:53
  798.9 103.7 %copy-start.1 = (f32[2048,128]{1,0:T(8,128)S(1)}, f32[2048,128]{1,0:T(8,128)}, u32[]{:S(2)}) copy-start(f32[2048,128]{1,0:T(8,128)} %get-tuple-element.21) | copy-start | bytes 3145732
Sparse Core Ops, SparseCore 0:
  212.9 53.1 all-reduce.5
  512.0 50.3 all-reduce.7
  809.6 50.3 all-reduce.9
